TPU v7x, 32 devices: a whole 2x2x4 slice. The times are simulated.
32 devices in a mesh: row: 8 (over y, x, core), col: 4 (over z).
Axes of the slice: x: 2, y: 2, z: 4, core: 2. Of those that a mesh axis runs over, the one named last changes fastest.
Arguments:
- row_geometry: float32 [4, 8, 16, 4, 2, 256], P('col', 'row'), may hold values from 0 to 1, as said below
- column_geometry: float32 [4, 2, 512], replicated, may hold values from 0 to 1
- octree_slot: int32 [4, 8, 8, 2], P('col'), may hold values from 0 to 15, as said below
- pivots: int32 [256], replicated, may hold values from 0 to 65535, as said below
- lower_inv: float32 [256, 256], replicated, as said below
- upper_inv: float32 [256, 256], replicated, as said below
Outputs:
- slab_out: float32 [8, 4, 8, 256, 512], P('row', 'col')
- upper_block: float32 [256, 256], replicated
Inputs may be any that keep to these rules, and one draw needn't show every extreme that they name: For each process column q and owner d, the entries octree_slot[q, :, d, :] are each local tile number 0 to 15 once. pivots[i] lies between i and 65535. `row_geometry`: the two tiles of one tile row carry equal row geometry in their slots. `lower_inv`: unit lower triangular. `upper_inv`: upper triangular with positive diagonal.
All inputs are finite; a program needn't handle non-finite values.
Results may differ from a plain program's by a relative error of at most 0.0003.
Values sent between devices are 32-bit elements; how exact they have to be, the bound alone decides.
No kernel may reach another device: no remote copies, remote signals or barrier semaphores. Data moves between devices by JAX's collectives and lax.ppermute only.
A program may use at most 64 MiB of HBM per device.

v0:
```python
import jax
import jax.numpy as jnp
from jax import lax
from jax.sharding import PartitionSpec as P

KAPPA = 9.0
SOFTEN = 0.05


def kernel_entries(row_points, column_points):
    quad_count = row_points.shape[-2]
    accumulated = None
    for row_point in range(quad_count):
        for column_point in range(quad_count):
            along_x = (
                row_points[..., 0, row_point, :, None]
                - column_points[..., 0, column_point, None, :]
            )
            along_y = (
                row_points[..., 1, row_point, :, None]
                - column_points[..., 1, column_point, None, :]
            )
            along_z = (
                row_points[..., 2, row_point, :, None]
                - column_points[..., 2, column_point, None, :]
            )
            spacing = jnp.sqrt(along_x * along_x + along_y * along_y + along_z * along_z)
            summand = (
                row_points[..., 3, row_point, :, None]
                * column_points[..., 3, column_point, None, :]
                * jnp.cos(KAPPA * spacing)
                / (spacing + SOFTEN)
            )
            accumulated = summand if accumulated is None else accumulated + summand
    return accumulated


def tracked_swaps(pivots):
    tile_size = pivots.shape[0]
    positions = jnp.concatenate([jnp.arange(tile_size, dtype=jnp.int32), pivots])
    same = positions[:, None] == positions[None, :]
    first_slot = jnp.argmax(same, axis=1)

    def advance(index_now, compact):
        slot_here = first_slot[index_now]
        slot_there = first_slot[index_now + tile_size]
        at_step = compact[slot_here]
        at_target = compact[slot_there]
        return compact.at[slot_here].set(at_target).at[slot_there].set(at_step)

    compact = lax.fori_loop(0, tile_size, advance, positions)
    values = jnp.take(compact, first_slot, axis=0)
    return (positions, values)


def per_device(row_geometry, column_geometry, octree_slot, pivots, lower_inv, upper_inv):
    row_count = lax.axis_size("row")
    col_count = lax.axis_size("col")
    row_place = lax.axis_index("row")
    col_place = lax.axis_index("col")
    tile_size = pivots.shape[0]
    slots_all = row_geometry.shape[2]
    tile_rows_dev = slots_all // 2
    quad_count = row_geometry.shape[4]
    fill_geometry = row_geometry[0, 0]
    slot_table = octree_slot[0]
    fill_tiles = lax.dynamic_index_in_dim(slot_table, row_place, 0, keepdims=False).reshape(-1)
    arrival = lax.dynamic_index_in_dim(slot_table, row_place, 1, keepdims=False).reshape(-1)
    placement_index = (
        jnp.zeros((slots_all,), jnp.int32).at[arrival].set(jnp.arange(slots_all, dtype=jnp.int32))
    )
    column_halves = column_geometry.reshape(4, quad_count, 2, tile_size)
    halves = jnp.take(column_halves, fill_tiles % 2, axis=2)
    filled = kernel_entries(fill_geometry, jnp.transpose(halves, (2, 0, 1, 3)))
    arrived = lax.all_to_all(filled, "row", split_axis=0, concat_axis=0, tiled=True)
    owned_tiles = jnp.take(arrived, placement_index, axis=0)
    slab_rows = (
        owned_tiles.reshape(tile_rows_dev, 2, tile_size, tile_size)
        .transpose(0, 2, 1, 3)
        .reshape(tile_rows_dev * tile_size, 2 * tile_size)
    )
    positions, values = tracked_swaps(pivots)
    local_tile_rows = row_place + row_count * (
        col_place + col_count * jnp.arange(tile_rows_dev, dtype=jnp.int32)
    )
    global_rows = (
        local_tile_rows[:, None] * tile_size + jnp.arange(tile_size, dtype=jnp.int32)[None, :]
    ).reshape(-1)
    matched = global_rows[:, None] == positions[None, :]
    found = jnp.max(jnp.where(matched, values[None, :], -1), axis=1)
    sources = jnp.where(found >= 0, found, global_rows)
    pivot_sources = values[:tile_size]
    source_tiles = pivot_sources // tile_size
    holds_row = (source_tiles % row_count == row_place) & (
        source_tiles // row_count % col_count == col_place
    )
    local_index = jnp.where(
        holds_row,
        source_tiles // (row_count * col_count) * tile_size + pivot_sources % tile_size,
        0,
    )
    pivot_part = jnp.where(holds_row[:, None], jnp.take(slab_rows, local_index, axis=0), 0.0)
    leading = (row_place == 0) & (col_place == 0)
    initial_part = jnp.where(leading, slab_rows[:tile_size], 0.0)
    initial_top, pivot_top = lax.psum((initial_part, pivot_part), ("row", "col"))
    from_pivots = jnp.take(pivot_top, jnp.minimum(global_rows, tile_size - 1), axis=0)
    from_initial = jnp.take(initial_top, jnp.minimum(sources, tile_size - 1), axis=0)
    permuted = jnp.where(
        (global_rows < tile_size)[:, None],
        from_pivots,
        jnp.where((sources == global_rows)[:, None], slab_rows, from_initial),
    )
    highest = lax.Precision.HIGHEST
    upper_block = jnp.dot(
        lower_inv, pivot_top[:, tile_size:], precision=highest, preferred_element_type=jnp.float32
    )
    lower_panel = jnp.dot(
        permuted[:, :tile_size], upper_inv, precision=highest, preferred_element_type=jnp.float32
    )
    trailing = permuted[:, tile_size:] - jnp.dot(
        lower_panel, upper_block, precision=highest, preferred_element_type=jnp.float32
    )
    slab_out = jnp.concatenate([lower_panel, trailing], axis=1).reshape(
        1, 1, tile_rows_dev, tile_size, 2 * tile_size
    )
    return (slab_out, upper_block)


def solution(mesh):
    placed = (
        P("col", "row", None, None, None, None),
        P(),
        P("col", None, None, None),
        P(),
        P(),
        P(),
    )
    return jax.shard_map(
        per_device,
        mesh=mesh,
        in_specs=placed,
        out_specs=(P("row", "col", None, None, None), P()),
        check_vma=False,
    )
```

profile of v0, /device:TPU:0, one launch (start us, length us, event | category | flops | bytes accessed | tf_op | source)
XLA Modules:
  0.0 1934.2 jit_solution(667069928864595273)
XLA Ops:
  8.2 1.0 dynamic-slice_reduce_fusion
  10.9 1.0 fusion.17
  12.0 153.8 %divide_add_fusion = f32[16,256,256]{2,1,0:T(8,128)} fusion(f32[16,256]{1,0:T(8,128)S(1)} %get-tuple-element.183, f32[16,256]{1,0:T(8,128)S(1)} %get-tuple-element.184, f32[16,256]{1,0:T(8,128)S(1)} %get-tuple-element.185, f32[16,256]{1,0:T(8,128)S(1)} %get-tuple-element.186, f32[16,256]{1,0:T(8,128)S(1)} %bitcast.101, f32[16,256]{1,0:T(8,128)S(1)} %bitcast.95, ...), kind=kLoop, calls=%fused_computation.14 | loop fusion | flops 57671680 | bytes 4456448 | tf_op jit(solution)/shard_map/add | solution.py:34
  165.8 5.3 all-to-all-start
  173.3 1534.3 %while.17 = (s32[]{:T(128)}, s32[512]{0:T(512)S(1)}, s32[512]{0:T(512)S(1)}, s32[]{:T(128)}, s32[]{:T(128)}, /*index=5*/s32[]{:T(128)}, s32[]{:T(128)}, s32[]{:T(128)}, s32[]{:T(128)}) while((s32[]{:T(128)}, s32[512]{0:T(512)S(1)}, s32[512]{0:T(512)S(1)}, s32[]{:T(128)}, s32[]{:T(128)}, /*index=5*/s32[]{:T(128)}, s32[]{:T(128)}, s32[]{:T(128)}, ...), condition=%wide.region_2.3_spmd, body=%wide.region_1.2_spmd.sunk | while | flops 20 | bytes 2363 | solution.py:51
  1707.5 3.5 gather_fusion
  1711.1 5.0 gather_fusion.2
  1716.2 4.7 select_bitcast_fusion
  1720.8 5.5 copy.39
  1726.4 1.1 slice_select_fusion
  1727.4 6.2 copy.64
  1734.8 5.3 copy.40
  1740.2 3.4 gather_fusion.3
  1745.5 132.6 %all-reduce.3.cloned.1.call-done = (f32[256,512]{1,0:T(8,128)}, f32[256,512]{1,0:T(8,128)}) async-done(((f32[256,512]{1,0:T(8,128)}, f32[256,512]{1,0:T(8,128)}), (f32[256,512]{1,0:T(8,128)}, f32[256,512]{1,0:T(8,128)})) %all-reduce.3.cloned.1.call-update) | async-done | bytes 1048592 | tf_op jit(solution)/shard_map/psum | solution.py:105
  1878.2 1.6 fusion.3
  1880.6 8.9 gather_fusion.4
  1889.5 5.4 copy.41
  1895.0 8.9 gather_fusion.5
  1903.9 5.4 copy.43
  1909.4 6.1 fusion
  1915.5 2.0 fusion.1
  1917.5 2.0 convolution_subtract_fusion
  1919.6 2.4 pad_maximum_fusion
  1922.0 5.3 copy.46
  (1087 shorter events, 676.4 us)
Async XLA Ops:
  7.2 1908.3 %copy-start = (f32[256,256]{1,0:T(8,128)S(1)}, f32[256,256]{1,0:T(8,128)}, u32[]{:S(2)}) copy-start(f32[256,256]{1,0:T(8,128)} %param.19) | copy-start | bytes 786436
  165.8 5.4 copy-start.4
  165.8 1545.3 %all-to-all-start = ((f32[16,256,256]{2,1,0:T(8,128)}), f32[16,256,256]{2,1,0:T(8,128)}, u32[]{:S(2)}, u32[]{:S(2)}) async-start(f32[16,256,256]{2,1,0:T(8,128)} %divide_add_fusion), calls=%async_computation | async-start | bytes 8388608 | tf_op jit(solution)/shard_map/all_to_all | solution.py:75
  171.2 1707.0 %all-reduce.3.cloned.1.call-start = ((), (), s32[]{:S(2)}) async-start(), calls=%async_computation.1 | async-start | bytes 2097152 | tf_op jit(solution)/shard_map/psum | solution.py:105
  1740.2 138.0 %copy-start.3 = (f32[256,256]{1,0:T(8,128)S(1)}, f32[256,256]{1,0:T(8,128)}, u32[]{:S(2)}) copy-start(f32[256,256]{1,0:T(8,128)} %param.18) | copy-start | bytes 786436
  1878.2 2.5 copy-start.1
  1889.5 5.5 copy-start.2
Sparse Core Ops, SparseCore 0:
  1744.7 133.3 all-reduce.2
where the time goes:
time: 1950 us; the launch traced here: 1930 us
  loops' own time  867 us (44%)
  other arithmetic  542 us (28%)
  local copies, waits for them, and re-layouts  367 us (19%)
  waiting for transfers between devices  133 us (7%)
    another operation x1, loops' own time, tracked_swaps(): compact = lax.fori_loop(0, tile_size, advance, positions)  867 us
    scatter x512, other arithmetic, advance(): return compact.at[slot_here].set(at_target).at[slot_there].set(at_step)  371 us
    add x1, other arithmetic, kernel_entries(): accumulated = summand if accumulated is None else accumulated + summand  154 us
    dynamic_slice x256, local copies, waits for them, and re-layouts, advance(): slot_there = first_slot[index_now + tile_size]  148 us
    another operation x256, local copies, waits for them, and re-layouts  148 us
    psum x1, waiting for transfers between devices, per_device(): lax.psum((initial_part, pivot_part), ('row', 'col'))  133 us
  transfers between devices with their start and end apart: 2, of which 1 were waited for; matrix products, arithmetic and copies ran while one was open for 35% of the time, Pallas kernels for 0%

commit v1 on v0

--- a/solution.py
+++ b/solution.py
@@ -102,7 +102,7 @@
     pivot_part = jnp.where(holds_row[:, None], jnp.take(slab_rows, local_index, axis=0), 0.0)
     leading = (row_place == 0) & (col_place == 0)
     initial_part = jnp.where(leading, slab_rows[:tile_size], 0.0)
-    initial_top, pivot_top = lax.psum((initial_part, pivot_part), ("row", "col"))
+    initial_top, pivot_top = lax.psum(lax.psum((initial_part, pivot_part), "col"), "row")
     from_pivots = jnp.take(pivot_top, jnp.minimum(global_rows, tile_size - 1), axis=0)
     from_initial = jnp.take(initial_top, jnp.minimum(sources, tile_size - 1), axis=0)
     permuted = jnp.where(

time: 1950 us -> 2110 us (1.082)
  loops' own time: 867 us -> 990 us
  local copies, waits for them, and re-layouts: 367 us -> 395 us
  other arithmetic: 542 us -> 568 us
    another operation x1, loops' own time: 867 us -> 990 us  [tracked_swaps(): compact = lax.fori_loop(0, tile_size, advance, positions)]
    scatter x512, other arithmetic: 371 us -> 396 us  [advance(): return compact.at[slot_here].set(at_target).at[slot_there].set(at_step)]
    psum x1 -> x2, waiting for transfers between devices: 133 us -> 112 us  [the longest x1 58.3 us: per_device(): lax.psum(lax.psum((initial_part, pivot_part), 'col'), 'row')]
  transfers between devices with their start and end apart: 2 -> 3, of which waited for: 1 -> 2; matrix products, arithmetic and copies ran while one was open for 35% -> 35% of each run, Pallas kernels for 0% -> 0%
where the time goes in v1:
time: 2110 us; the launch traced here: 2090 us
  loops' own time  990 us (47%)
  other arithmetic  568 us (27%)
  local copies, waits for them, and re-layouts  395 us (19%)
  waiting for transfers between devices  112 us (5%)
    another operation x1, loops' own time, tracked_swaps(): compact = lax.fori_loop(0, tile_size, advance, positions)  990 us
    scatter x512, other arithmetic, advance(): return compact.at[slot_here].set(at_target).at[slot_there].set(at_step)  396 us
    dynamic_slice x256, local copies, waits for them, and re-layouts, advance(): slot_there = first_slot[index_now + tile_size]  166 us
    another operation x256, local copies, waits for them, and re-layouts  158 us
    add x1, other arithmetic, kernel_entries(): accumulated = summand if accumulated is None else accumulated + summand  154 us
    psum x1, waiting for transfers between devices, per_device(): lax.psum(lax.psum((initial_part, pivot_part), 'col'), 'row')  58.3 us
    psum x1, waiting for transfers between devices, per_device(): lax.psum((initial_part, pivot_part), 'col')  54.1 us
  transfers between devices with their start and end apart: 3, of which 2 were waited for; matrix products, arithmetic and copies ran while one was open for 35% of the time, Pallas kernels for 0%

profile of v1, /device:TPU:0, one launch (start us, length us, event | category | flops | bytes accessed | tf_op | source)
XLA Modules:
  0.0 2090.7 jit_solution(8806377221871084311)
XLA Ops:
  12.0 153.9 %divide_add_fusion = f32[16,256,256]{2,1,0:T(8,128)} fusion(f32[16,256]{1,0:T(8,128)S(1)} %get-tuple-element.185, f32[16,256]{1,0:T(8,128)S(1)} %get-tuple-element.186, f32[16,256]{1,0:T(8,128)S(1)} %get-tuple-element.187, f32[16,256]{1,0:T(8,128)S(1)} %get-tuple-element.188, f32[16,256]{1,0:T(8,128)S(1)} %bitcast.101, f32[16,256]{1,0:T(8,128)S(1)} %bitcast.95, ...), kind=kLoop, calls=%fused_computation.14 | loop fusion | flops 57671680 | bytes 4456448 | tf_op jit(solution)/shard_map/add | solution.py:34
  165.9 5.3 all-to-all-start
  172.3 1.0 iota_reduce_fusion
  173.3 1710.4 %while.17 = (s32[]{:T(128)}, s32[512]{0:T(512)S(1)}, s32[512]{0:T(512)S(1)}, s32[]{:T(128)}, s32[]{:T(128)}, /*index=5*/s32[]{:T(128)}, s32[]{:T(128)}, s32[]{:T(128)}, s32[]{:T(128)}) while((s32[]{:T(128)}, s32[512]{0:T(512)S(1)}, s32[512]{0:T(512)S(1)}, s32[]{:T(128)}, s32[]{:T(128)}, /*index=5*/s32[]{:T(128)}, s32[]{:T(128)}, s32[]{:T(128)}, ...), condition=%wide.region_2.3_spmd, body=%wide.region_1.2_spmd.sunk | while | flops 20 | bytes 2363 | solution.py:51
  1883.7 3.5 gather_fusion
  1887.3 5.0 gather_fusion.2
  1892.3 4.7 select_bitcast_fusion
  1897.0 5.5 copy.39
  1902.5 1.1 slice_select_fusion
  1903.6 6.2 copy.64
  1911.0 5.3 copy.40
  1916.4 3.4 gather_fusion.3
  1921.1 54.1 %all-reduce.7.cloned.1.call-done = (f32[256,512]{1,0:T(8,128)}, f32[256,512]{1,0:T(8,128)}) async-done(((f32[256,512]{1,0:T(8,128)}, f32[256,512]{1,0:T(8,128)}), (f32[256,512]{1,0:T(8,128)}, f32[256,512]{1,0:T(8,128)})) %all-reduce.7.cloned.1.call-update) | async-done | bytes 1048592 | tf_op jit(solution)/shard_map/psum | solution.py:105
  1976.2 58.3 %all-reduce.5.cloned.1.call-done = (f32[256,512]{1,0:T(8,128)}, f32[256,512]{1,0:T(8,128)}) async-done(((f32[256,512]{1,0:T(8,128)}, f32[256,512]{1,0:T(8,128)}), (f32[256,512]{1,0:T(8,128)}, f32[256,512]{1,0:T(8,128)})) %all-reduce.5.cloned.1.call-update) | async-done | bytes 1048592 | tf_op jit(solution)/shard_map/psum | solution.py:105
  2034.6 1.6 fusion.3
  2037.0 9.0 gather_fusion.4
  2046.0 5.5 copy.41
  2051.5 8.9 gather_fusion.5
  2060.4 5.5 copy.43
  2065.8 6.1 fusion
  2072.0 2.1 fusion.1
  2074.0 2.1 convolution_subtract_fusion
  2076.1 2.4 pad_maximum_fusion
  2078.5 5.3 copy.46
  (1090 shorter events, 730.5 us)
Async XLA Ops:
  7.2 2064.8 %copy-start = (f32[256,256]{1,0:T(8,128)S(1)}, f32[256,256]{1,0:T(8,128)}, u32[]{:S(2)}) copy-start(f32[256,256]{1,0:T(8,128)} %param.19) | copy-start | bytes 786436
  165.9 5.4 copy-start.4
  165.9 1721.4 %all-to-all-start = ((f32[16,256,256]{2,1,0:T(8,128)}), f32[16,256,256]{2,1,0:T(8,128)}, u32[]{:S(2)}, u32[]{:S(2)}) async-start(f32[16,256,256]{2,1,0:T(8,128)} %divide_add_fusion), calls=%async_computation | async-start | bytes 8388608 | tf_op jit(solution)/shard_map/all_to_all | solution.py:75
  171.2 1804.0 %all-reduce.7.cloned.1.call-start = ((), (), s32[]{:S(2)}) async-start(), calls=%async_computation.2 | async-start | bytes 2097152 | tf_op jit(solution)/shard_map/psum | solution.py:105
  1916.4 118.2 %copy-start.3 = (f32[256,256]{1,0:T(8,128)S(1)}, f32[256,256]{1,0:T(8,128)}, u32[]{:S(2)}) copy-start(f32[256,256]{1,0:T(8,128)} %param.18) | copy-start | bytes 786436
  1920.8 113.8 %all-reduce.5.cloned.1.call-start = ((), (), s32[]{:S(2)}) async-start(), calls=%async_computation.1 | async-start | bytes 2097152 | tf_op jit(solution)/shard_map/psum | solution.py:105
  2034.5 2.5 copy-start.1
  2046.0 5.5 copy-start.2
Sparse Core Ops, SparseCore 0:
  1920.9 54.3 all-reduce.6
  1978.5 56.0 all-reduce.4
